TPU v7x, 256 devices: a whole 4x4x8 slice. The times are simulated.
256 devices in a mesh: ctx: 32 (over z_lo, y, x), head: 8 (over z_hi, core).
Axes of the slice: x: 4, y: 4, z: 8 (z_hi: 4, z_lo: 2; z = z_hi * 2 + z_lo), core: 2. Of those that a mesh axis runs over, the one named last changes fastest.
Arguments:
- queries: bfloat16 [8192, 5120], P('ctx', 'head'), may hold values from -800 to 800
- keys: bfloat16 [8192, 5120], P('ctx', 'head'), may hold values from -800 to 800
- values: bfloat16 [8192, 5120], P('ctx', 'head'), may hold values from -6 to 6
- q_gain: float32 [5120], P('head'), may hold values from 0.6 to 1.5
- k_gain: float32 [5120], P('head'), may hold values from 0.6 to 1.5
- ref_keys: bfloat16 [32768, 5120], P('ctx', 'head'), may hold values from -6 to 6
- ref_values: bfloat16 [32768, 5120], P('ctx', 'head'), may hold values from -6 to 6
- out_weight: bfloat16 [5120, 5120], P('head'), may hold values from -0.078125 to 0.078125
- partners: int32 [32, 2, 12], replicated, may hold values from 0 to 63, as said below
- owners: int32 [2], replicated, may hold values from 0 to 31, as said below
- labels: int32 [64], P('ctx'), may hold values from 0 to 1
Outputs:
- attended: bfloat16 [8192, 5120], P('ctx', 'head')
- mixed: bfloat16 [8192, 5120], P('ctx', 'head')
Inputs may be any that keep to these rules, and one draw needn't show every extreme that they name: `partners`: over both persons' lists of one context shard, the blocks of any one shard are named at most 1 times, and the blocks of some shard exactly 1 times. `owners`: the persons' identity shards differ, and one of them is the last shard.
All inputs are finite; a program needn't handle non-finite values.
Results may differ from a plain program's by a relative error of at most 0.018.
Values may be sent and summed in bfloat16 or wider, within the bound.
A program may use at most 128 MiB of HBM per device.

v0:
```python
import jax
import jax.numpy as jnp
from jax import lax
from jax.sharding import PartitionSpec as P

D = 5120
HD = 128
BLK = 128
epsilon = 1e-06


def spread(value, axis, source):
    kept = jnp.where(lax.axis_index(axis) == source, value, 0).astype(value.dtype)
    return lax.psum(kept, axis)


def normalize(features, scale_gain, square_total):
    factor = lax.rsqrt(square_total / D + epsilon)
    return (features * factor[:, None] * scale_gain[None, :]).astype(jnp.bfloat16)


def attend_block(query, own_keys, own_values, far_keys, far_values, bank_keys, bank_values):
    row_count, width = query.shape
    head_count = width // HD
    key_set = jnp.concatenate([own_keys, far_keys, bank_keys], axis=0)
    value_set = jnp.concatenate([own_values, far_values, bank_values], axis=0)
    query_heads = query.reshape(row_count, head_count, HD)
    key_heads = key_set.reshape(-1, head_count, HD)
    value_heads = value_set.reshape(-1, head_count, HD)
    scores = jnp.einsum(
        "qhd,khd->hqk", query_heads, key_heads, preferred_element_type=jnp.float32
    ) * HD ** (-0.5)
    row_peak = jnp.max(scores, axis=2, keepdims=True)
    exponent = jnp.exp(scores - row_peak)
    denominator = jnp.sum(exponent, axis=2)
    weights = exponent.astype(jnp.bfloat16)
    combined = jnp.einsum("hqk,khd->qhd", weights, value_heads, preferred_element_type=jnp.float32)
    return (combined / denominator.T[:, :, None]).reshape(row_count, width).astype(jnp.bfloat16)


def shards(
    queries,
    keys,
    values,
    q_gain,
    k_gain,
    ref_keys,
    ref_values,
    out_weight,
    partners,
    owners,
    labels,
):
    tokens, width = queries.shape
    blocks = tokens // BLK
    own_index = lax.axis_index("ctx")
    persons = partners.shape[1]
    q_float = queries.astype(jnp.float32)
    k_float = keys.astype(jnp.float32)
    q_total, k_total = lax.psum(
        (jnp.sum(q_float * q_float, axis=1), jnp.sum(k_float * k_float, axis=1)), "head"
    )
    q_norm = normalize(q_float, q_gain, q_total)
    k_norm = normalize(k_float, k_gain, k_total)
    query_blocks = q_norm.reshape(blocks, BLK, width)
    key_blocks = k_norm.reshape(blocks, BLK, width)
    value_blocks = values.reshape(blocks, BLK, width)
    wanted = partners[own_index].reshape(-1)
    whole_keys, whole_values = (
        lax.all_gather(k_norm, "ctx", axis=0, tiled=True),
        lax.all_gather(values, "ctx", axis=0, tiled=True),
    )
    far_keys = whole_keys.reshape(-1, BLK, width)[wanted]
    far_values = whole_values.reshape(-1, BLK, width)[wanted]
    far_keys = far_keys.reshape(persons, -1, width)
    far_values = far_values.reshape(persons, -1, width)
    local_bank = jnp.stack([ref_keys, ref_values])
    identities = []
    for person in range(persons):
        identities.append(spread(local_bank, "ctx", owners[person]))
    identity_stack = jnp.stack(identities)

    def one_block(position):
        person_label = labels[position]
        return attend_block(
            query_blocks[position],
            key_blocks[position],
            value_blocks[position],
            far_keys[person_label],
            far_values[person_label],
            identity_stack[person_label, 0],
            identity_stack[person_label, 1],
        )

    attended = lax.map(one_block, jnp.arange(blocks)).reshape(tokens, width)
    partial_out = jnp.dot(attended, out_weight, preferred_element_type=jnp.float32)
    mixed = lax.psum_scatter(
        partial_out.astype(jnp.bfloat16), "head", scatter_dimension=1, tiled=True
    )
    return (attended, mixed)


def solution(mesh):
    return jax.shard_map(
        shards,
        mesh=mesh,
        in_specs=(
            P("ctx", "head"),
            P("ctx", "head"),
            P("ctx", "head"),
            P("head"),
            P("head"),
            P("ctx", "head"),
            P("ctx", "head"),
            P("head", None),
            P(),
            P(),
            P("ctx"),
        ),
        out_specs=(P("ctx", "head"), P("ctx", "head")),
        check_vma=False,
    )
```

profile of v0, /device:TPU:28, one launch (start us, length us, event | category | flops | bytes accessed | tf_op | source)
XLA Modules:
  0.0 848.1 jit_solution(13434496772358359575)
XLA Ops:
  9.8 1.6 copy.45
  11.5 1.6 copy.46
  13.1 2.8 select_bitcast_fusion.1
  17.1 19.9 %all-reduce = (f32[256]{0:T(256)S(1)}, f32[256]{0:T(256)S(1)}) all-reduce(f32[256]{0:T(256)S(1)} %get-tuple-element.121, f32[256]{0:T(256)S(1)} %get-tuple-element.122), channel_id=1, replica_groups=mesh['ctx'=32,'head'=8] {'head'}, use_global_device_ids=true, to_apply=%region_1.0 | all-reduce | flops 512 | bytes 4096 | tf_op jit(solution)/shard_map/psum | solution.py:60
  40.0 308.8 %all-reduce.4.cloned.1.call-done = (bf16[1,2,1024,640]{2,3,1,0:T(8,128)(2,1)}, bf16[1,2,1024,640]{2,3,1,0:T(8,128)(2,1)}) async-done(((bf16[1,2,1024,640]{2,3,1,0:T(8,128)(2,1)}, bf16[1,2,1024,640]{2,3,1,0:T(8,128)(2,1)}), (bf16[1,2,1024,640]{2,3,1,0:T(8,128)(2,1)}, bf16[1,2,1024,640]{2,3,1,0:T(8,128)(2,1)})) %all-reduce.4.cloned.1.call-update) | async-done | bytes 5242896 | tf_op jit(solution)/shard_map/psum | solution.py:14
  348.8 5.3 pad_maximum_fusion
  354.1 169.4 %all-gather.5.cloned.1.call-done = bf16[8192,640]{1,0:T(8,128)(2,1)} async-done(((bf16[256,640]{1,0:T(8,128)(2,1)}), bf16[8192,640]{1,0:T(8,128)(2,1)}) %all-gather.5.cloned.1.call-update) | async-done | bytes 10485776 | tf_op jit(solution)/shard_map/all_gather | solution.py:70
  523.5 7.2 gather_fusion.1
  530.8 166.6 %all-gather.3.cloned.1.call-done = bf16[8192,640]{1,0:T(8,128)(2,1)} async-done(((bf16[256,640]{1,0:T(8,128)(2,1)}), bf16[8192,640]{1,0:T(8,128)(2,1)}) %all-gather.3.cloned.1.call-update) | async-done | bytes 10485776 | tf_op jit(solution)/shard_map/all_gather | solution.py:71
  697.4 7.2 gather_fusion
  704.7 75.3 %while.10 = (s32[]{:T(128)}, bf16[2,128,640]{2,1,0:T(8,128)(2,1)}, s32[2]{0:T(128)S(1)}, bf16[2,128,640]{2,1,0:T(8,128)(2,1)}, s32[2]{0:T(128)S(1)}, /*index=5*/...) while((s32[]{:T(128)}, bf16[2,128,640]{2,1,0:T(8,128)(2,1)}, ...), condition=%wide.region_9.10_spmd, body=%wide.region_6.9_spmd.sunk | while | flops 915372800 | bytes 109458328 | solution.py:95
  709.7 4.4 constant_dynamic-slice_fusion.14
  714.1 2.7 copy.74
  716.8 2.3 copy.75
  719.1 3.0 constant_dynamic-slice_fusion.13
  722.1 1.5 copy.73
  725.1 4.5 multiply_reduce_fusion.2
  730.9 1.7 copy-done.3
  732.7 2.4 copy.78
  736.2 5.1 fusion.55
  747.3 4.4 constant_dynamic-slice_fusion.14
  751.8 2.7 copy.74
  754.5 2.3 copy.75
  756.7 3.0 constant_dynamic-slice_fusion.13
  762.8 4.5 multiply_reduce_fusion.2
  768.5 1.7 copy-done.3
  770.3 2.4 copy.78
  773.8 5.1 fusion.55
  779.9 5.2 convolution_convert_fusion
  785.1 2.6 copy.54
  787.8 52.0 %reduce-scatter.4.cloned.1.call-done = bf16[640,256]{1,0:T(8,128)(2,1)} async-done(((bf16[5120,256]{1,0:T(8,128)(2,1)}), bf16[640,256]{1,0:T(8,128)(2,1)}) %reduce-scatter.4.cloned.1.call-update) | async-done | bytes 327696
  839.7 1.9 copy.55
  (80 shorter events, 19.0 us)
Async XLA Ops:
  7.2 31.6 %copy-start = (s32[32,2,12]{0,1,2:T(2,128)S(1)}, s32[32,2,12]{0,1,2:T(2,128)}, u32[]{:S(2)}) copy-start(s32[32,2,12]{0,1,2:T(2,128)} %param.21) | copy-start | bytes 9220
  7.2 341.6 %all-reduce.4.cloned.1.call-start = ((), (), s32[]{:S(2)}) async-start(), calls=%async_computation.4 | async-start | bytes 10485760 | tf_op jit(solution)/shard_map/psum | solution.py:14
  15.8 1.0 copy-start.6
  15.8 1.1 copy-start.7
  15.8 21.2 %copy-start.8 = (f32[640]{0:T(1024)S(1)}, f32[640]{0:T(1024)}, u32[]{:S(2)}) copy-start(f32[640]{0:T(1024)} %param.17) | copy-start | bytes 7684
  15.8 23.2 %copy-start.9 = (f32[640]{0:T(1024)S(1)}, f32[640]{0:T(1024)}, u32[]{:S(2)}) copy-start(f32[640]{0:T(1024)} %param.16) | copy-start | bytes 7684
  15.9 507.7 %all-gather.5.cloned.1.call-start = ((), (), s32[]{:S(2)}) async-start(), calls=%async_computation.2 | async-start | bytes 10813440 | tf_op jit(solution)/shard_map/all_gather | solution.py:70
  38.0 659.4 %all-gather.3.cloned.1.call-start = ((), (), s32[]{:S(2)}) async-start(), calls=%async_computation.1 | async-start | bytes 10813440 | tf_op jit(solution)/shard_map/all_gather | solution.py:71
  38.7 801.0 %reduce-scatter.4.cloned.1.call-start = ((), (), s32[]{:S(2)}) async-start(), calls=%async_computation.3 | async-start | bytes 2949120
  697.4 7.3 copy-start.12
  722.1 3.0 copy-start.4
  729.6 3.0 copy-start.3
  729.6 3.0 copy-start.2
  732.6 3.6 copy-start.5
  736.2 5.3 copy-start.10
  741.6 0.7 copy-start.11
  759.7 3.0 copy-start.4
  767.3 3.0 copy-start.3
  767.3 3.0 copy-start.2
  770.3 3.6 copy-start.5
  773.8 5.3 copy-start.10
  779.2 0.7 copy-start.11
  779.9 61.7 %copy-start.1 = (s32[32,2,12]{0,1,2:T(2,128)S(1)}, s32[32,2,12]{0,1,2:T(2,128)}, u32[]{:S(2)}) copy-start(s32[32,2,12]{0,1,2:T(2,128)} %param.21) | copy-start | bytes 9220
Sparse Core Ops, SparseCore 0:
  16.0 332.7 all-reduce.3
  350.5 172.9 all-gather.4
  525.3 172.0 all-gather.2
  787.9 51.7 reduce-scatter.3
where the time goes:
time: 849 us; the launch traced here: 848 us
  waiting for transfers between devices  698 us (82%)
  local copies, waits for them, and re-layouts  70.4 us (8%)
  matrix products  24.5 us (3%)
  blocking collectives  19.9 us (2%)
  between operations  15.2 us (2%)
  other arithmetic  12.6 us (1%)
    psum x1, waiting for transfers between devices, spread(): return lax.psum(kept, axis)  309 us
    all_gather x1, waiting for transfers between devices, shards(): lax.all_gather(k_norm, 'ctx', axis=0, tiled=True)  169 us
    all_gather x1, waiting for transfers between devices, shards(): lax.all_gather(values, 'ctx', axis=0, tiled=True)  167 us
    unnamed x5, waiting for transfers between devices  52.7 us
    psum x1, blocking collectives, shards(): lax.psum((jnp.sum(q_float * q_float, axis=1), jnp.sum(k_float * k_float,...  19.9 us
  transfers between devices with their start and end apart: 4, of which 4 were waited for; matrix products, arithmetic and copies ran while one was open for 2% of the time, Pallas kernels for 0%

commit v1 on v0

--- a/solution.py
+++ b/solution.py
@@ -67,7 +67,15 @@
     value_blocks = values.reshape(blocks, BLK, width)
     wanted = partners[own_index].reshape(-1)
     whole_keys, whole_values = (
-        lax.all_gather(k_norm, "ctx", axis=0, tiled=True),
+        jnp.concatenate(
+            lax.all_to_all(
+                jnp.stack(lax.axis_size("ctx") * [k_norm], axis=0),
+                axis_name="ctx",
+                split_axis=0,
+                concat_axis=0,
+            ),
+            0,
+        ),
         lax.all_gather(values, "ctx", axis=0, tiled=True),
     )
     far_keys = whole_keys.reshape(-1, BLK, width)[wanted]

time: 849 us -> 789 us (0.929)
  waiting for transfers between devices: 698 us -> 623 us
    all_gather x1 -> x0, waiting for transfers between devices: 169 us -> none  [shards(): lax.all_gather(k_norm, 'ctx', axis=0, tiled=True)]
    psum x1, waiting for transfers between devices: 309 us -> 409 us  [spread(): return lax.psum(kept, axis)]
    unnamed x5 -> x4, waiting for transfers between devices: 52.7 us -> 52 us
  transfers between devices with their start and end apart: 4 -> 4, of which waited for: 4 -> 3; matrix products, arithmetic and copies ran while one was open for 2% -> 3% of each run, Pallas kernels for 0% -> 0%
where the time goes in v1:
time: 789 us; the launch traced here: 787 us
  waiting for transfers between devices  623 us (79%)
  local copies, waits for them, and re-layouts  76.6 us (10%)
  matrix products  24.5 us (3%)
  blocking collectives  19.9 us (3%)
  between operations  15.1 us (2%)
  other arithmetic  12.6 us (2%)
  starting transfers between devices  8.32 us (1%)
    psum x1, waiting for transfers between devices, spread(): return lax.psum(kept, axis)  409 us
    all_gather x1, waiting for transfers between devices, shards(): lax.all_gather(values, 'ctx', axis=0, tiled=True)  162 us
    unnamed x4, waiting for transfers between devices  52 us
    psum x1, blocking collectives, shards(): lax.psum((jnp.sum(q_float * q_float, axis=1), jnp.sum(k_float * k_float,...  19.9 us
  transfers between devices with their start and end apart: 4, of which 3 were waited for; matrix products, arithmetic and copies ran while one was open for 3% of the time, Pallas kernels for 0%

profile of v1, /device:TPU:28, one launch (start us, length us, event | category | flops | bytes accessed | tf_op | source)
XLA Modules:
  0.0 787.3 jit_solution(3925018044978311522)
XLA Ops:
  9.8 1.6 copy.45
  11.5 1.6 copy.46
  13.1 2.7 select_bitcast_fusion.1
  17.0 19.9 %all-reduce = (f32[256]{0:T(256)S(1)}, f32[256]{0:T(256)S(1)}) all-reduce(f32[256]{0:T(256)S(1)} %fusion.35, f32[256]{0:T(256)S(1)} %fusion.38), channel_id=1, replica_groups=mesh['ctx'=32,'head'=8] {'head'}, use_global_device_ids=true, to_apply=%region_1.0 | all-reduce | flops 512 | bytes 4096 | tf_op jit(solution)/shard_map/psum | solution.py:60
  37.9 6.3 stack.20
  44.2 8.0 %all-to-all-start = ((bf16[32,256,640]{2,1,0:T(8,128)(2,1)}), bf16[32,256,640]{2,1,0:T(8,128)(2,1)}, u32[]{:S(2)}, u32[]{:S(2)}) async-start(bf16[32,256,640]{2,1,0:T(8,128)(2,1)} %stack.20), calls=%async_computation | async-start | bytes 20971520 | tf_op jit(solution)/shard_map/all_to_all | solution.py:71
  54.4 409.0 %all-reduce.4.cloned.1.call-done = (bf16[1,2,1024,640]{2,3,1,0:T(8,128)(2,1)}, bf16[1,2,1024,640]{2,3,1,0:T(8,128)(2,1)}) async-done(((bf16[1,2,1024,640]{2,3,1,0:T(8,128)(2,1)}, bf16[1,2,1024,640]{2,3,1,0:T(8,128)(2,1)}), (bf16[1,2,1024,640]{2,3,1,0:T(8,128)(2,1)}, bf16[1,2,1024,640]{2,3,1,0:T(8,128)(2,1)})) %all-reduce.4.cloned.1.call-update) | async-done | bytes 5242896 | tf_op jit(solution)/shard_map/psum | solution.py:14
  463.4 5.3 pad_maximum_fusion
  468.7 7.1 gather_fusion.1
  475.9 162.3 %all-gather.2.cloned.1.call-done = bf16[8192,640]{1,0:T(8,128)(2,1)} async-done(((bf16[256,640]{1,0:T(8,128)(2,1)}), bf16[8192,640]{1,0:T(8,128)(2,1)}) %all-gather.2.cloned.1.call-update) | async-done | bytes 10485776 | tf_op jit(solution)/shard_map/all_gather | solution.py:79
  638.2 7.2 gather_fusion
  645.4 74.4 %while.10 = (s32[]{:T(128)}, bf16[2,128,640]{2,1,0:T(8,128)(2,1)}, s32[2]{0:T(128)S(1)}, bf16[2,128,640]{2,1,0:T(8,128)(2,1)}, s32[2]{0:T(128)S(1)}, /*index=5*/...) while((s32[]{:T(128)}, bf16[2,128,640]{2,1,0:T(8,128)(2,1)}, ...), condition=%wide.region_9.10_spmd, body=%wide.region_6.9_spmd.sunk | while | flops 915372800 | bytes 109458328 | solution.py:103
  649.9 4.5 constant_dynamic-slice_fusion.14
  654.4 2.7 copy.74
  657.1 2.3 copy.75
  659.5 3.0 constant_dynamic-slice_fusion.13
  665.5 4.5 multiply_reduce_fusion.2
  671.3 1.7 copy-done.3
  673.0 2.4 copy.78
  676.5 5.1 fusion.55
  687.1 4.5 constant_dynamic-slice_fusion.14
  691.7 2.7 copy.74
  694.4 2.3 copy.75
  696.7 3.0 constant_dynamic-slice_fusion.13
  702.7 4.5 multiply_reduce_fusion.2
  708.5 1.7 copy-done.3
  710.2 2.4 copy.78
  713.7 5.1 fusion.55
  719.8 5.2 convolution_convert_fusion
  725.0 2.6 copy.54
  727.6 51.2 %reduce-scatter.4.cloned.1.call-done = bf16[640,256]{1,0:T(8,128)(2,1)} async-done(((bf16[5120,256]{1,0:T(8,128)(2,1)}), bf16[640,256]{1,0:T(8,128)(2,1)}) %reduce-scatter.4.cloned.1.call-update) | async-done | bytes 327696
  778.9 1.9 copy.55
  (80 shorter events, 20.6 us)
Async XLA Ops:
  7.2 46.1 %copy-start = (s32[32,2,12]{0,1,2:T(2,128)S(1)}, s32[32,2,12]{0,1,2:T(2,128)}, u32[]{:S(2)}) copy-start(s32[32,2,12]{0,1,2:T(2,128)} %param.21) | copy-start | bytes 9220
  7.2 456.3 %all-reduce.4.cloned.1.call-start = ((), (), s32[]{:S(2)}) async-start(), calls=%async_computation.4 | async-start | bytes 10485760 | tf_op jit(solution)/shard_map/psum | solution.py:14
  15.8 1.0 copy-start.7
  15.8 1.1 copy-start.6
  15.8 21.2 %copy-start.8 = (f32[640]{0:T(1024)S(1)}, f32[640]{0:T(1024)}, u32[]{:S(2)}) copy-start(f32[640]{0:T(1024)} %param.17) | copy-start | bytes 7684
  44.2 9.3 %copy-start.9 = (f32[640]{0:T(1024)S(1)}, f32[640]{0:T(1024)}, u32[]{:S(2)}) copy-start(f32[640]{0:T(1024)} %param.16) | copy-start | bytes 7684
  44.2 424.5 %all-to-all-start = ((bf16[32,256,640]{2,1,0:T(8,128)(2,1)}), bf16[32,256,640]{2,1,0:T(8,128)(2,1)}, u32[]{:S(2)}, u32[]{:S(2)}) async-start(bf16[32,256,640]{2,1,0:T(8,128)(2,1)} %stack.20), calls=%async_computation | async-start | bytes 20971520 | tf_op jit(solution)/shard_map/all_to_all | solution.py:71
  52.3 585.9 %all-gather.2.cloned.1.call-start = ((), (), s32[]{:S(2)}) async-start(), calls=%async_computation.2 | async-start | bytes 10813440 | tf_op jit(solution)/shard_map/all_gather | solution.py:79
  53.0 725.8 %reduce-scatter.4.cloned.1.call-start = ((), (), s32[]{:S(2)}) async-start(), calls=%async_computation.3 | async-start | bytes 2949120
  638.2 7.2 copy-start.12
  662.5 3.0 copy-start.4
  670.0 3.0 copy-start.3
  670.0 3.0 copy-start.2
  673.0 3.5 copy-start.5
  676.5 5.3 copy-start.10
  681.9 0.7 copy-start.11
  699.7 3.0 copy-start.4
  707.2 3.0 copy-start.3
  707.2 3.0 copy-start.2
  710.2 3.5 copy-start.5
  713.7 5.3 copy-start.10
  719.1 0.7 copy-start.11
  719.8 60.9 %copy-start.1 = (s32[32,2,12]{0,1,2:T(2,128)S(1)}, s32[32,2,12]{0,1,2:T(2,128)}, u32[]{:S(2)}) copy-start(s32[32,2,12]{0,1,2:T(2,128)} %param.21) | copy-start | bytes 9220
Sparse Core Ops, SparseCore 0:
  15.9 447.4 all-reduce.3
  465.2 172.9 all-gather.1
  727.8 51.0 reduce-scatter.3
